TPU v7x, 256 devices: a whole 4x4x8 slice. The times are simulated.
256 devices in a mesh: gx: 16 (over y, z_lo, core), gy: 4 (over x), gz: 4 (over z_hi).
Axes of the slice: x: 4, y: 4, z: 8 (z_hi: 4, z_lo: 2; z = z_hi * 2 + z_lo), core: 2. Of those that a mesh axis runs over, the one named last changes fastest.
Arguments:
- features: bfloat16 [32, 64, 16, 1024], P(None, 'gx', 'gy', 'gz'), may hold values from -6 to 6
- conv_one: bfloat16 [32, 864], replicated, may hold values from -0.3125 to 0.3125
- conv_two: bfloat16 [32, 864], replicated, may hold values from -0.3125 to 0.3125
- conv_three: bfloat16 [64, 864], replicated, may hold values from -0.3125 to 0.3125
- conv_four: bfloat16 [64, 1728], replicated, may hold values from -0.21875 to 0.21875
- depth_one: bfloat16 [64, 27], replicated, may hold values from -1.25 to 1.25
- point_one: bfloat16 [128, 64], replicated, may hold values from -1 to 1
- depth_two: bfloat16 [128, 27], replicated, may hold values from -1.25 to 1.25
- point_two: bfloat16 [128, 128], replicated, may hold values from -0.75 to 0.75
- conv_five: bfloat16 [64, 5184], replicated, may hold values from -0.125 to 0.125
- conv_six: bfloat16 [32, 2592], replicated, may hold values from -0.125 to 0.125
Outputs:
- decoded: bfloat16 [32, 64, 16, 1024], P(None, 'gx', 'gy', 'gz')
All inputs are finite; a program needn't handle non-finite values.
Results may differ from a plain program's by a relative error of at most 0.015.
Values may be sent and summed in bfloat16 or wider, within the bound.
No kernel may reach another device: no remote copies, remote signals or barrier semaphores. Data moves between devices by JAX's collectives and lax.ppermute only.
A program may use at most 64 MiB of HBM per device.

v0:
```python
import jax
import jax.numpy as jnp
from jax import lax
from jax.sharding import PartitionSpec as P


def padded_2(cells, sides, width):
    for axis, dim in sides:
        count = lax.axis_size(axis)
        ends = count - 1
        head = lax.slice_in_dim(cells, 0, width, axis=dim)
        tail = lax.slice_in_dim(cells, cells.shape[dim] - width, cells.shape[dim], axis=dim)
        cells = jnp.concatenate(
            [
                lax.ppermute(tail, axis, [(i, (i + 1) % count) for i in range(ends)]),
                cells,
                lax.ppermute(head, axis, [((i + 1) % count, i) for i in range(ends)]),
            ],
            axis=dim,
        )
    return cells


def rectify(values):
    return jnp.maximum(values, 0.0)


def pad_faces(values):
    return padded_2(values, (("gx", 1), ("gy", 2), ("gz", 3)), 1)


def convolve(padded, weight):
    channels = padded.shape[0]
    width_out = weight.shape[0]
    size_x = padded.shape[1] - 2
    size_y = padded.shape[2] - 2
    size_z = padded.shape[3] - 2
    volume = size_x * size_y * size_z
    summed = jnp.zeros((width_out, volume), jnp.float32)
    for offset_x in range(3):
        for offset_y in range(3):
            for offset_z in range(3):
                tap_index = (offset_x * 3 + offset_y) * 3 + offset_z
                piece = padded[
                    :,
                    offset_x : offset_x + size_x,
                    offset_y : offset_y + size_y,
                    offset_z : offset_z + size_z,
                ].reshape(channels, volume)
                columns = weight[:, tap_index * channels : (tap_index + 1) * channels]
                summed = summed + jnp.dot(columns, piece, preferred_element_type=jnp.float32)
    return summed.reshape(width_out, size_x, size_y, size_z)


def depthwise(padded, tap_weights):
    size_x = padded.shape[1] - 2
    size_y = padded.shape[2] - 2
    size_z = padded.shape[3] - 2
    summed = jnp.zeros((padded.shape[0], size_x, size_y, size_z), jnp.float32)
    for offset_x in range(3):
        for offset_y in range(3):
            for offset_z in range(3):
                tap_index = (offset_x * 3 + offset_y) * 3 + offset_z
                factor = tap_weights[:, tap_index].astype(jnp.float32)[:, None, None, None]
                window = padded[
                    :,
                    offset_x : offset_x + size_x,
                    offset_y : offset_y + size_y,
                    offset_z : offset_z + size_z,
                ]
                summed = summed + window.astype(jnp.float32) * factor
    return summed.astype(jnp.bfloat16)


def shrink(values):
    channels, size_x, size_y, size_z = values.shape
    return values.reshape(channels, size_x // 2, 2, size_y // 2, 2, size_z // 2, 2).max(
        axis=(2, 4, 6)
    )


def enlarge(values):
    channels, size_x, size_y, size_z = values.shape
    grown = jnp.broadcast_to(
        values[:, :, None, :, None, :, None], (channels, size_x, 2, size_y, 2, size_z, 2)
    )
    return grown.reshape(channels, 2 * size_x, 2 * size_y, 2 * size_z)


def conv_pair(values, weight_a, weight_b):
    middle = rectify(convolve(pad_faces(values), weight_a)).astype(jnp.bfloat16)
    return rectify(convolve(pad_faces(middle), weight_b)).astype(jnp.bfloat16)


def channel_depthwise(values, tap_weights):
    channels, size_x, size_y, size_z = values.shape
    planes = lax.axis_size(("gx", "gy"))
    rows_x = lax.axis_size("gx")
    rows_y = lax.axis_size("gy")
    per_device = channels // planes
    volume = size_x * size_y * size_z
    outgoing = values.reshape(1, channels, volume)
    arrived = lax.all_to_all(outgoing, ("gx", "gy"), split_axis=1, concat_axis=0, tiled=True)
    arranged = arrived.reshape(rows_x, rows_y, per_device, size_x, size_y, size_z).transpose(
        2, 0, 3, 1, 4, 5
    )
    arranged = arranged.reshape(per_device, rows_x * size_x, rows_y * size_y, size_z)
    rimmed = padded_2(arranged, (("gz", 3),), 1)
    padded = jnp.pad(rimmed, ((0, 0), (1, 1), (1, 1), (0, 0)))
    own_taps = lax.dynamic_slice_in_dim(
        tap_weights, lax.axis_index(("gx", "gy")) * per_device, per_device, 0
    )
    spread = depthwise(padded, own_taps)
    outgoing_back = spread.reshape(per_device, rows_x, size_x, rows_y, size_y, size_z).transpose(
        1, 3, 0, 2, 4, 5
    )
    outgoing_back = outgoing_back.reshape(planes, per_device, volume)
    returned = lax.all_to_all(outgoing_back, ("gx", "gy"), split_axis=0, concat_axis=1, tiled=True)
    return returned.reshape(channels, size_x, size_y, size_z)


def quarter_layer(values, tap_weights, mixing):
    channels, size_x, size_y, size_z = values.shape
    spread = channel_depthwise(values, tap_weights)
    flattened = spread.reshape(channels, size_x * size_y * size_z)
    mixed_out = rectify(jnp.dot(mixing, flattened, preferred_element_type=jnp.float32))
    return mixed_out.astype(jnp.bfloat16).reshape(mixing.shape[0], size_x, size_y, size_z)


def decoder_input(coarse, fine_skip):
    return pad_faces(jnp.concatenate([enlarge(coarse), fine_skip], axis=0))


def local(
    features,
    conv_one,
    conv_two,
    conv_three,
    conv_four,
    depth_one,
    point_one,
    depth_two,
    point_two,
    conv_five,
    conv_six,
):
    skip = conv_pair(features, conv_one, conv_two)
    half_in = shrink(skip)
    half_skip = conv_pair(half_in, conv_three, conv_four)
    quarter = shrink(half_skip)
    mixed_one = quarter_layer(quarter, depth_one, point_one)
    mixed_two = quarter_layer(mixed_one, depth_two, point_two)
    half_out = rectify(convolve(decoder_input(mixed_two, half_skip), conv_five)).astype(
        jnp.bfloat16
    )
    return convolve(decoder_input(half_out, skip), conv_six).astype(jnp.bfloat16)


def solution(mesh):
    in_specs = (P(None, "gx", "gy", "gz"), P(), P(), P(), P(), P(), P(), P(), P(), P(), P())
    out_specs = P(None, "gx", "gy", "gz")
    return jax.shard_map(local, mesh=mesh, in_specs=in_specs, out_specs=out_specs, check_vma=False)
```

profile of v0, /device:TPU:72, one launch (start us, length us, event | category | flops | bytes accessed | tf_op | source)
XLA Modules:
  0.0 486.0 jit_solution(7746145017843126168)
XLA Ops:
  2.9 4.5 collective-permute-start.1
  19.6 4.5 collective-permute-done.3
  27.8 6.0 %collective-permute-start.4 = (bf16[32,6,6,1]{3,2,1,0:T(8,128)(2,1)}, bf16[32,6,6,1]{3,2,1,0:T(8,128)(2,1)}, u32[]{:S(2)}, u32[]{:S(2)}) collective-permute-start(bf16[32,6,6,1]{3,2,1,0:T(8,128)(2,1)} %get-tuple-element.112), channel_id=1, source_target_pairs={{0,1},{1,2},{2,3},{4,5},{5,6},{6,7},{8,9},{9,10},{10,11},{12,13},{... | collective-permute-start | bytes 6920 | tf_op jit(solution)/shard_map/ppermute | solution.py:15
  40.0 9.7 %collective-permute-done.5 = bf16[32,6,6,1]{3,2,1,0:T(8,128)(2,1)} collective-permute-done((bf16[32,6,6,1]{3,2,1,0:T(8,128)(2,1)}, bf16[32,6,6,1]{3,2,1,0:T(8,128)(2,1)}, u32[]{:S(2)}, u32[]{:S(2)}) %collective-permute-start.5) | collective-permute-done | bytes 2336 | tf_op jit(solution)/shard_map/ppermute | solution.py:17
  99.3 4.5 collective-permute-start.7
  120.5 5.6 %collective-permute-start.10 = (bf16[32,6,6,1]{3,2,1,0:T(8,128)(2,1)}, bf16[32,6,6,1]{3,2,1,0:T(8,128)(2,1)}, u32[]{:S(2)}, u32[]{:S(2)}) collective-permute-start(bf16[32,6,6,1]{3,2,1,0:T(8,128)(2,1)} %get-tuple-element.107), channel_id=1, source_target_pairs={{0,1},{1,2},{2,3},{4,5},{5,6},{6,7},{8,9},{9,10},{10,11},{12,13},{... | collective-permute-start | bytes 6920 | tf_op jit(solution)/shard_map/ppermute | solution.py:15
  141.3 6.6 %collective-permute-done.11 = bf16[32,6,6,1]{3,2,1,0:T(8,128)(2,1)} collective-permute-done((bf16[32,6,6,1]{3,2,1,0:T(8,128)(2,1)}, bf16[32,6,6,1]{3,2,1,0:T(8,128)(2,1)}, u32[]{:S(2)}, u32[]{:S(2)}) %collective-permute-start.11) | collective-permute-done | bytes 2336 | tf_op jit(solution)/shard_map/ppermute | solution.py:17
  205.8 4.5 collective-permute-start.13
  229.3 5.0 %collective-permute-done.17 = bf16[32,4,4,1]{3,0,2,1:T(8,128)(2,1)S(1)} collective-permute-done((bf16[32,4,4,1]{3,0,2,1:T(8,128)(2,1)S(1)}, bf16[32,4,4,1]{3,0,2,1:T(8,128)(2,1)S(1)}, u32[]{:S(2)}, u32[]{:S(2)}) %collective-permute-start.17) | collective-permute-done | bytes 1056 | tf_op jit(solution)/shard_map/ppermute | solution.py:17
  242.2 4.5 collective-permute-start.19
  261.9 5.1 %collective-permute-start.23 = (bf16[64,4,4,1]{3,2,1,0:T(4,128)(2,1)S(1)}, bf16[64,4,4,1]{3,2,1,0:T(4,128)(2,1)S(1)}, u32[]{:S(2)}, u32[]{:S(2)}) collective-permute-start(bf16[64,4,4,1]{3,2,1,0:T(4,128)(2,1)S(1)} %get-tuple-element.170), channel_id=1, source_target_pairs={{1,0},{2,1},{3,2},{5,4},{6,5},{7,6},{9,8},{10,9},{11,10},{13,12},{... | collective-permute-start | bytes 6152 | tf_op jit(solution)/shard_map/ppermute | solution.py:17
  270.8 7.8 %collective-permute-done.23 = bf16[64,4,4,1]{3,2,1,0:T(4,128)(2,1)S(1)} collective-permute-done((bf16[64,4,4,1]{3,2,1,0:T(4,128)(2,1)S(1)}, bf16[64,4,4,1]{3,2,1,0:T(4,128)(2,1)S(1)}, u32[]{:S(2)}, u32[]{:S(2)}) %collective-permute-start.23) | collective-permute-done | bytes 2080 | tf_op jit(solution)/shard_map/ppermute | solution.py:17
  323.2 4.8 collective-permute-start.25
  332.2 8.4 %all-to-all-start.1 = ((bf16[64,1,64]{2,1,0:T(2,128)(2,1)}), bf16[64,1,64]{2,1,0:T(2,128)(2,1)S(1)}, u32[]{:S(2)}, u32[]{:S(2)}) async-start(bf16[64,1,64]{2,1,0:T(2,128)(2,1)} %copy.374), calls=%async_computation.1 | async-start | bytes 65536 | tf_op jit(solution)/shard_map/all_to_all | solution.py:118
  340.6 7.0 %all-to-all-done.1 = bf16[64,1,64]{2,1,0:T(2,128)(2,1)S(1)} async-done(((bf16[64,1,64]{2,1,0:T(2,128)(2,1)}), bf16[64,1,64]{2,1,0:T(2,128)(2,1)S(1)}, u32[]{:S(2)}, u32[]{:S(2)}) %all-to-all-start.1) | async-done | bytes 8224 | tf_op jit(solution)/shard_map/all_to_all | solution.py:118
  348.5 5.6 %all-to-all-start.2 = ((bf16[1,128,64]{2,0,1:T(2,128)(2,1)}), bf16[1,128,64]{2,0,1:T(2,128)(2,1)S(1)}, u32[]{:S(2)}, u32[]{:S(2)}) async-start(bf16[1,128,64]{2,0,1:T(2,128)(2,1)} %copy.375), calls=%async_computation.2 | async-start | bytes 131072 | tf_op jit(solution)/shard_map/all_to_all | solution.py:103
  354.3 7.0 %all-to-all-done.2 = bf16[1,128,64]{2,0,1:T(2,128)(2,1)S(1)} async-done(((bf16[1,128,64]{2,0,1:T(2,128)(2,1)}), bf16[1,128,64]{2,0,1:T(2,128)(2,1)S(1)}, u32[]{:S(2)}, u32[]{:S(2)}) %all-to-all-start.2) | async-done | bytes 16416 | tf_op jit(solution)/shard_map/all_to_all | solution.py:103
  363.3 4.8 collective-permute-start.27
  372.2 12.2 %all_to_all.16 = bf16[64,2,64]{2,1,0:T(2,128)(2,1)S(1)} all-to-all(bf16[64,2,64]{2,1,0:T(2,128)(2,1)S(1)} %copy.378), channel_id=1, replica_groups=mesh['gx'=16,'gy'=4,'gz'=4] {'gx','gy'}, dimensions={0} | all-to-all | bytes 32768 | tf_op jit(solution)/shard_map/all_to_all | solution.py:118
  386.6 4.5 collective-permute-start.29
  410.0 4.3 collective-permute-start.32
  427.0 4.5 collective-permute-start.35
  441.1 5.6 %collective-permute-done.36 = bf16[96,6,1,256]{0,3,2,1:T(8,128)(2,1)S(1)} collective-permute-done((bf16[96,6,1,256]{0,3,2,1:T(8,128)(2,1)S(1)}, bf16[96,6,1,256]{0,3,2,1:T(8,128)(2,1)S(1)}, u32[]{:S(2)}, u32[]{:S(2)}) %collective-permute-start.36) | collective-permute-done | bytes 294944 | tf_op jit(solution)/shard_map/ppermute | solution.py:15
  451.1 5.5 %collective-permute-start.38 = (bf16[96,6,6,1]{0,3,2,1:T(2,128)(2,1)S(1)}, bf16[96,6,6,1]{0,3,2,1:T(2,128)(2,1)S(1)}, u32[]{:S(2)}, u32[]{:S(2)}) collective-permute-start(bf16[96,6,6,1]{0,3,2,1:T(2,128)(2,1)S(1)} %get-tuple-element.7), channel_id=1, source_target_pairs={{0,1},{1,2},{2,3},{4,5},{5,6},{6,7},{8,9},{9,10},{10,11},{12,13},{... | collective-permute-start | bytes 20744 | tf_op jit(solution)/shard_map/ppermute | solution.py:15
  (581 shorter events, 323.1 us)
Async XLA Ops:
  11.1 8.5 %collective-permute-start.2 = (bf16[32,6,1,256]{3,2,1,0:T(2,128)(2,1)S(1)}, bf16[32,6,1,256]{3,2,1,0:T(2,128)(2,1)S(1)}, u32[]{:S(2)}, u32[]{:S(2)}) collective-permute-start(bf16[32,6,1,256]{3,2,1,0:T(2,128)(2,1)S(1)} %get-tuple-element.157), channel_id=1, source_target_pairs={{0,4},{4,8},{8,12},{1,5},{5,9},{9,13},{2,6},{6,10},{10,14},{3,7},{... | collective-permute-start | bytes 294920 | tf_op jit(solution)/shard_map/ppermute | solution.py:15
  14.5 9.6 %collective-permute-start.3 = (bf16[32,6,1,256]{3,2,1,0:T(2,128)(2,1)S(1)}, bf16[32,6,1,256]{3,2,1,0:T(2,128)(2,1)S(1)}, u32[]{:S(2)}, u32[]{:S(2)}) collective-permute-start(bf16[32,6,1,256]{3,2,1,0:T(2,128)(2,1)S(1)} %get-tuple-element.158), channel_id=1, source_target_pairs={{4,0},{8,4},{12,8},{5,1},{9,5},{13,9},{6,2},{10,6},{14,10},{7,3},{... | collective-permute-start | bytes 294920 | tf_op jit(solution)/shard_map/ppermute | solution.py:17
  25.9 23.8 %collective-permute-start.5 = (bf16[32,6,6,1]{3,2,1,0:T(8,128)(2,1)}, bf16[32,6,6,1]{3,2,1,0:T(8,128)(2,1)}, u32[]{:S(2)}, u32[]{:S(2)}) collective-permute-start(bf16[32,6,6,1]{3,2,1,0:T(8,128)(2,1)} %get-tuple-element.111), channel_id=1, source_target_pairs={{1,0},{2,1},{3,2},{5,4},{6,5},{7,6},{9,8},{10,9},{11,10},{13,12},{... | collective-permute-start | bytes 6920 | tf_op jit(solution)/shard_map/ppermute | solution.py:17
  27.8 22.5 %collective-permute-start.4 = (bf16[32,6,6,1]{3,2,1,0:T(8,128)(2,1)}, bf16[32,6,6,1]{3,2,1,0:T(8,128)(2,1)}, u32[]{:S(2)}, u32[]{:S(2)}) collective-permute-start(bf16[32,6,6,1]{3,2,1,0:T(8,128)(2,1)} %get-tuple-element.112), channel_id=1, source_target_pairs={{0,1},{1,2},{2,3},{4,5},{5,6},{6,7},{8,9},{9,10},{10,11},{12,13},{... | collective-permute-start | bytes 6920 | tf_op jit(solution)/shard_map/ppermute | solution.py:15
  106.6 8.1 %collective-permute-start.8 = (bf16[32,6,1,256]{3,2,1,0:T(2,128)(2,1)S(1)}, bf16[32,6,1,256]{3,2,1,0:T(2,128)(2,1)S(1)}, u32[]{:S(2)}, u32[]{:S(2)}) collective-permute-start(bf16[32,6,1,256]{3,2,1,0:T(2,128)(2,1)S(1)} %get-tuple-element.152), channel_id=1, source_target_pairs={{0,4},{4,8},{8,12},{1,5},{5,9},{9,13},{2,6},{6,10},{10,14},{3,7},{... | collective-permute-start | bytes 294920 | tf_op jit(solution)/shard_map/ppermute | solution.py:15
  110.0 8.8 %collective-permute-start.9 = (bf16[32,6,1,256]{3,2,1,0:T(2,128)(2,1)S(1)}, bf16[32,6,1,256]{3,2,1,0:T(2,128)(2,1)S(1)}, u32[]{:S(2)}, u32[]{:S(2)}) collective-permute-start(bf16[32,6,1,256]{3,2,1,0:T(2,128)(2,1)S(1)} %get-tuple-element.153), channel_id=1, source_target_pairs={{4,0},{8,4},{12,8},{5,1},{9,5},{13,9},{6,2},{10,6},{14,10},{7,3},{... | collective-permute-start | bytes 294920 | tf_op jit(solution)/shard_map/ppermute | solution.py:17
  120.5 20.8 %collective-permute-start.10 = (bf16[32,6,6,1]{3,2,1,0:T(8,128)(2,1)}, bf16[32,6,6,1]{3,2,1,0:T(8,128)(2,1)}, u32[]{:S(2)}, u32[]{:S(2)}) collective-permute-start(bf16[32,6,6,1]{3,2,1,0:T(8,128)(2,1)} %get-tuple-element.107), channel_id=1, source_target_pairs={{0,1},{1,2},{2,3},{4,5},{5,6},{6,7},{8,9},{9,10},{10,11},{12,13},{... | collective-permute-start | bytes 6920 | tf_op jit(solution)/shard_map/ppermute | solution.py:15
  126.1 21.8 %collective-permute-start.11 = (bf16[32,6,6,1]{3,2,1,0:T(8,128)(2,1)}, bf16[32,6,6,1]{3,2,1,0:T(8,128)(2,1)}, u32[]{:S(2)}, u32[]{:S(2)}) collective-permute-start(bf16[32,6,6,1]{3,2,1,0:T(8,128)(2,1)} %get-tuple-element.108), channel_id=1, source_target_pairs={{1,0},{2,1},{3,2},{5,4},{6,5},{7,6},{9,8},{10,9},{11,10},{13,12},{... | collective-permute-start | bytes 6920 | tf_op jit(solution)/shard_map/ppermute | solution.py:17
  221.4 7.9 %collective-permute-start.16 = (bf16[32,4,4,1]{3,0,2,1:T(8,128)(2,1)S(1)}, bf16[32,4,4,1]{3,0,2,1:T(8,128)(2,1)S(1)}, u32[]{:S(2)}, u32[]{:S(2)}) collective-permute-start(bf16[32,4,4,1]{3,0,2,1:T(8,128)(2,1)S(1)} %get-tuple-element.206), channel_id=1, source_target_pairs={{0,1},{1,2},{2,3},{4,5},{5,6},{6,7},{8,9},{9,10},{10,11},{12,13},{... | collective-permute-start | bytes 3080 | tf_op jit(solution)/shard_map/ppermute | solution.py:15
  224.7 9.6 %collective-permute-start.17 = (bf16[32,4,4,1]{3,0,2,1:T(8,128)(2,1)S(1)}, bf16[32,4,4,1]{3,0,2,1:T(8,128)(2,1)S(1)}, u32[]{:S(2)}, u32[]{:S(2)}) collective-permute-start(bf16[32,4,4,1]{3,0,2,1:T(8,128)(2,1)S(1)} %get-tuple-element.207), channel_id=1, source_target_pairs={{1,0},{2,1},{3,2},{5,4},{6,5},{7,6},{9,8},{10,9},{11,10},{13,12},{... | collective-permute-start | bytes 3080 | tf_op jit(solution)/shard_map/ppermute | solution.py:17
  259.8 11.0 %collective-permute-start.22 = (bf16[64,4,4,1]{3,2,1,0:T(4,128)(2,1)}, bf16[64,4,4,1]{3,2,1,0:T(4,128)(2,1)S(1)}, u32[]{:S(2)}, u32[]{:S(2)}) collective-permute-start(bf16[64,4,4,1]{3,2,1,0:T(4,128)(2,1)} %get-tuple-element.169), channel_id=1, source_target_pairs={{0,1},{1,2},{2,3},{4,5},{5,6},{6,7},{8,9},{9,10},{10,11},{12,13},{... | collective-permute-start | bytes 6152 | tf_op jit(solution)/shard_map/ppermute | solution.py:15
  261.9 16.8 %collective-permute-start.23 = (bf16[64,4,4,1]{3,2,1,0:T(4,128)(2,1)S(1)}, bf16[64,4,4,1]{3,2,1,0:T(4,128)(2,1)S(1)}, u32[]{:S(2)}, u32[]{:S(2)}) collective-permute-start(bf16[64,4,4,1]{3,2,1,0:T(4,128)(2,1)S(1)} %get-tuple-element.170), channel_id=1, source_target_pairs={{1,0},{2,1},{3,2},{5,4},{6,5},{7,6},{9,8},{10,9},{11,10},{13,12},{... | collective-permute-start | bytes 6152 | tf_op jit(solution)/shard_map/ppermute | solution.py:17
  298.9 22.3 %all-to-all-start = ((bf16[1,64,64]{2,0,1:T(2,128)(2,1)}), bf16[1,64,64]{2,0,1:T(2,128)(2,1)S(1)}, u32[]{:S(2)}, u32[]{:S(2)}) async-start(bf16[1,64,64]{2,0,1:T(2,128)(2,1)} %copy.373), calls=%async_computation | async-start | bytes 65536 | tf_op jit(solution)/shard_map/all_to_all | solution.py:103
  332.2 15.4 %all-to-all-start.1 = ((bf16[64,1,64]{2,1,0:T(2,128)(2,1)}), bf16[64,1,64]{2,1,0:T(2,128)(2,1)S(1)}, u32[]{:S(2)}, u32[]{:S(2)}) async-start(bf16[64,1,64]{2,1,0:T(2,128)(2,1)} %copy.374), calls=%async_computation.1 | async-start | bytes 65536 | tf_op jit(solution)/shard_map/all_to_all | solution.py:118
  348.5 12.7 %all-to-all-start.2 = ((bf16[1,128,64]{2,0,1:T(2,128)(2,1)}), bf16[1,128,64]{2,0,1:T(2,128)(2,1)S(1)}, u32[]{:S(2)}, u32[]{:S(2)}) async-start(bf16[1,128,64]{2,0,1:T(2,128)(2,1)} %copy.375), calls=%async_computation.2 | async-start | bytes 131072 | tf_op jit(solution)/shard_map/all_to_all | solution.py:103
  363.3 8.3 %collective-permute-start.27 = (bf16[2,16,4,1]{3,1,2,0:T(8,128)(2,1)S(1)}, bf16[2,16,4,1]{3,1,2,0:T(8,128)(2,1)S(1)}, u32[]{:S(2)}, u32[]{:S(2)}) collective-permute-start(bf16[2,16,4,1]{3,1,2,0:T(8,128)(2,1)S(1)} %get-tuple-element.226), channel_id=1, source_target_pairs={{1,0},{2,1},{3,2},{5,4},{6,5},{7,6},{9,8},{10,9},{11,10},{13,12},{... | collective-permute-start | bytes 776 | tf_op jit(solution)/shard_map/ppermute | solution.py:17
  393.8 8.3 %collective-permute-start.30 = (bf16[192,4,1,128]{0,3,2,1:T(8,128)(2,1)S(1)}, bf16[192,4,1,128]{0,3,2,1:T(8,128)(2,1)S(1)}, u32[]{:S(2)}, u32[]{:S(2)}) collective-permute-start(bf16[192,4,1,128]{0,3,2,1:T(8,128)(2,1)S(1)} %get-tuple-element.127), channel_id=1, source_target_pairs={{0,4},{4,8},{8,12},{1,5},{5,9},{9,13},{2,6},{6,10},{10,14},{3,7},{... | collective-permute-start | bytes 589832 | tf_op jit(solution)/shard_map/ppermute | solution.py:15
  396.3 10.0 %collective-permute-start.31 = (bf16[192,4,1,128]{0,3,2,1:T(8,128)(2,1)S(1)}, bf16[192,4,1,128]{0,3,2,1:T(8,128)(2,1)S(1)}, u32[]{:S(2)}, u32[]{:S(2)}) collective-permute-start(bf16[192,4,1,128]{0,3,2,1:T(8,128)(2,1)S(1)} %get-tuple-element.128), channel_id=1, source_target_pairs={{4,0},{8,4},{12,8},{5,1},{9,5},{13,9},{6,2},{10,6},{14,10},{7,3},{... | collective-permute-start | bytes 589832 | tf_op jit(solution)/shard_map/ppermute | solution.py:17
  406.4 8.6 %collective-permute-start.33 = (bf16[192,4,4,1]{0,2,3,1:T(4,128)(2,1)S(1)}, bf16[192,4,4,1]{0,2,3,1:T(4,128)(2,1)S(1)}, u32[]{:S(2)}, u32[]{:S(2)}) collective-permute-start(bf16[192,4,4,1]{0,2,3,1:T(4,128)(2,1)S(1)} %copy.384), channel_id=1, source_target_pairs={{1,0},{2,1},{3,2},{5,4},{6,5},{7,6},{9,8},{10,9},{11,10},{13,12},{... | collective-permute-start | bytes 18440 | tf_op jit(solution)/shard_map/ppermute | solution.py:17
  425.1 9.5 %collective-permute-start.34 = (bf16[96,1,4,256]{0,3,2,1:T(8,128)(2,1)S(1)}, bf16[96,1,4,256]{0,3,2,1:T(8,128)(2,1)S(1)}, u32[]{:S(2)}, u32[]{:S(2)}) collective-permute-start(bf16[96,1,4,256]{0,3,2,1:T(8,128)(2,1)S(1)} %get-tuple-element.33), channel_id=1, source_target_pairs={{0,16},{16,32},{32,48},{48,64},{64,80},{80,96},{96,112},{112,128},... | collective-permute-start | bytes 589832 | tf_op jit(solution)/shard_map/ppermute | solution.py:15
  427.0 8.4 %collective-permute-start.35 = (bf16[96,1,4,256]{0,3,2,1:T(8,128)(2,1)S(1)}, bf16[96,1,4,256]{0,3,2,1:T(8,128)(2,1)S(1)}, u32[]{:S(2)}, u32[]{:S(2)}) collective-permute-start(bf16[96,1,4,256]{0,3,2,1:T(8,128)(2,1)S(1)} %get-tuple-element.34), channel_id=1, source_target_pairs={{16,0},{32,16},{48,32},{64,48},{80,64},{96,80},{112,96},{128,112},... | collective-permute-start | bytes 589832 | tf_op jit(solution)/shard_map/ppermute | solution.py:17
  435.8 10.9 %collective-permute-start.36 = (bf16[96,6,1,256]{0,3,2,1:T(8,128)(2,1)S(1)}, bf16[96,6,1,256]{0,3,2,1:T(8,128)(2,1)S(1)}, u32[]{:S(2)}, u32[]{:S(2)}) collective-permute-start(bf16[96,6,1,256]{0,3,2,1:T(8,128)(2,1)S(1)} %get-tuple-element.11), channel_id=1, source_target_pairs={{0,4},{4,8},{8,12},{1,5},{5,9},{9,13},{2,6},{6,10},{10,14},{3,7},{... | collective-permute-start | bytes 884744 | tf_op jit(solution)/shard_map/ppermute | solution.py:15
  438.3 12.6 %collective-permute-start.37 = (bf16[96,6,1,256]{0,3,2,1:T(8,128)(2,1)S(1)}, bf16[96,6,1,256]{0,3,2,1:T(8,128)(2,1)S(1)}, u32[]{:S(2)}, u32[]{:S(2)}) collective-permute-start(bf16[96,6,1,256]{0,3,2,1:T(8,128)(2,1)S(1)} %get-tuple-element.12), channel_id=1, source_target_pairs={{4,0},{8,4},{12,8},{5,1},{9,5},{13,9},{6,2},{10,6},{14,10},{7,3},{... | collective-permute-start | bytes 884744 | tf_op jit(solution)/shard_map/ppermute | solution.py:17
  451.1 12.3 %collective-permute-start.38 = (bf16[96,6,6,1]{0,3,2,1:T(2,128)(2,1)S(1)}, bf16[96,6,6,1]{0,3,2,1:T(2,128)(2,1)S(1)}, u32[]{:S(2)}, u32[]{:S(2)}) collective-permute-start(bf16[96,6,6,1]{0,3,2,1:T(2,128)(2,1)S(1)} %get-tuple-element.7), channel_id=1, source_target_pairs={{0,1},{1,2},{2,3},{4,5},{5,6},{6,7},{8,9},{9,10},{10,11},{12,13},{... | collective-permute-start | bytes 20744 | tf_op jit(solution)/shard_map/ppermute | solution.py:15
  (80 other events, 942.8 us)
where the time goes:
time: 496 us; the launch traced here: 486 us
  starting transfers between devices  141 us (28%)
  waiting for transfers between devices  106 us (21%)
  local copies, waits for them, and re-layouts  104 us (21%)
  matrix products  71.7 us (14%)
  other arithmetic  30.6 us (6%)
  between operations  20 us (4%)
  blocking collectives  12.2 us (2%)
    dot_general x162, matrix products, convolve(): jnp.dot(columns, piece, preferred_element_type=jnp.float32)  71.3 us
    ppermute x20, waiting for transfers between devices, padded_2(): lax.ppermute(head, axis, [((i + 1) % count, i) for i in range(ends)])  70.4 us
    reshape x105, local copies, waits for them, and re-layouts, convolve(): piece = padded[:, offset_x:offset_x + size_x, offset_y:offset_y + size_y,...  69.7 us
    ppermute x20, starting transfers between devices, padded_2(): lax.ppermute(head, axis, [((i + 1) % count, i) for i in range(ends)])  63.2 us
    ppermute x20, starting transfers between devices, padded_2(): lax.ppermute(tail, axis, [(i, (i + 1) % count) for i in range(ends)])  59.5 us
    concatenate x25, other arithmetic, padded_2(): jnp.concatenate([lax.ppermute(tail, axis, [(i, (i + 1) % count) for i in...  25.9 us
    ppermute x20, waiting for transfers between devices, padded_2(): lax.ppermute(tail, axis, [(i, (i + 1) % count) for i in range(ends)])  21.8 us
    slice x43, local copies, waits for them, and re-layouts, convolve(): padded[:, offset_x:offset_x + size_x, offset_y:offset_y + size_y, offset_...  19 us
  transfers between devices with their start and end apart: 43, of which 34 were waited for; matrix products, arithmetic and copies ran while one was open for 7% of the time, Pallas kernels for 0%

commit v1 on v0

--- a/solution.py
+++ b/solution.py
@@ -115,7 +115,15 @@
         1, 3, 0, 2, 4, 5
     )
     outgoing_back = outgoing_back.reshape(planes, per_device, volume)
-    returned = lax.all_to_all(outgoing_back, ("gx", "gy"), split_axis=0, concat_axis=1, tiled=True)
+    returned = jnp.concatenate(
+        lax.all_to_all(
+            jnp.stack(jnp.split(outgoing_back, lax.axis_size(("gx", "gy")), axis=0)),
+            ("gx", "gy"),
+            0,
+            0,
+        ),
+        axis=1,
+    )
     return returned.reshape(channels, size_x, size_y, size_z)
 
 

time: 496 us -> 537 us (1.083)
  local copies, waits for them, and re-layouts: 104 us -> 139 us
    unnamed x127 -> x241, local copies, waits for them, and re-layouts: 3.73 us -> 36.6 us
where the time goes in v1:
time: 537 us; the launch traced here: 527 us
  starting transfers between devices  141 us (26%)
  local copies, waits for them, and re-layouts  139 us (26%)
  waiting for transfers between devices  107 us (20%)
  matrix products  76.3 us (14%)
  other arithmetic  31.3 us (6%)
  between operations  20.5 us (4%)
  blocking collectives  12.1 us (2%)
    dot_general x162, matrix products, convolve(): jnp.dot(columns, piece, preferred_element_type=jnp.float32)  75.9 us
    reshape x105, local copies, waits for them, and re-layouts, convolve(): piece = padded[:, offset_x:offset_x + size_x, offset_y:offset_y + size_y,...  71.7 us
    ppermute x20, waiting for transfers between devices, padded_2(): lax.ppermute(head, axis, [((i + 1) % count, i) for i in range(ends)])  69.5 us
    ppermute x20, starting transfers between devices, padded_2(): lax.ppermute(head, axis, [((i + 1) % count, i) for i in range(ends)])  63.4 us
    ppermute x20, starting transfers between devices, padded_2(): lax.ppermute(tail, axis, [(i, (i + 1) % count) for i in range(ends)])  59.5 us
    unnamed x241, local copies, waits for them, and re-layouts  36.6 us
    concatenate x25, other arithmetic, padded_2(): jnp.concatenate([lax.ppermute(tail, axis, [(i, (i + 1) % count) for i in...  26.6 us
    ppermute x20, waiting for transfers between devices, padded_2(): lax.ppermute(tail, axis, [(i, (i + 1) % count) for i in range(ends)])  23.2 us
  transfers between devices with their start and end apart: 43, of which 34 were waited for; matrix products, arithmetic and copies ran while one was open for 7% of the time, Pallas kernels for 0%

profile of v1, /device:TPU:72, one launch (start us, length us, event | category | flops | bytes accessed | tf_op | source)
XLA Modules:
  0.0 526.9 jit_solution(5012515438667076121)
XLA Ops:
  2.9 4.5 collective-permute-start.1
  19.6 4.5 collective-permute-done.3
  27.8 6.0 %collective-permute-start.4 = (bf16[32,6,6,1]{3,2,1,0:T(8,128)(2,1)}, bf16[32,6,6,1]{3,2,1,0:T(8,128)(2,1)}, u32[]{:S(2)}, u32[]{:S(2)}) collective-permute-start(bf16[32,6,6,1]{3,2,1,0:T(8,128)(2,1)} %get-tuple-element.112), channel_id=1, source_target_pairs={{0,1},{1,2},{2,3},{4,5},{5,6},{6,7},{8,9},{9,10},{10,11},{12,13},{... | collective-permute-start | bytes 6920 | tf_op jit(solution)/shard_map/ppermute | solution.py:15
  40.8 8.9 %collective-permute-done.5 = bf16[32,6,6,1]{3,2,1,0:T(8,128)(2,1)} collective-permute-done((bf16[32,6,6,1]{3,2,1,0:T(8,128)(2,1)}, bf16[32,6,6,1]{3,2,1,0:T(8,128)(2,1)}, u32[]{:S(2)}, u32[]{:S(2)}) %collective-permute-start.5) | collective-permute-done | bytes 2336 | tf_op jit(solution)/shard_map/ppermute | solution.py:17
  102.0 4.5 collective-permute-start.7
  123.2 5.6 %collective-permute-start.10 = (bf16[32,6,6,1]{3,2,1,0:T(8,128)(2,1)}, bf16[32,6,6,1]{3,2,1,0:T(8,128)(2,1)}, u32[]{:S(2)}, u32[]{:S(2)}) collective-permute-start(bf16[32,6,6,1]{3,2,1,0:T(8,128)(2,1)} %get-tuple-element.107), channel_id=1, source_target_pairs={{0,1},{1,2},{2,3},{4,5},{5,6},{6,7},{8,9},{9,10},{10,11},{12,13},{... | collective-permute-start | bytes 6920 | tf_op jit(solution)/shard_map/ppermute | solution.py:15
  144.0 6.6 %collective-permute-done.11 = bf16[32,6,6,1]{3,2,1,0:T(8,128)(2,1)} collective-permute-done((bf16[32,6,6,1]{3,2,1,0:T(8,128)(2,1)}, bf16[32,6,6,1]{3,2,1,0:T(8,128)(2,1)}, u32[]{:S(2)}, u32[]{:S(2)}) %collective-permute-start.11) | collective-permute-done | bytes 2336 | tf_op jit(solution)/shard_map/ppermute | solution.py:17
  212.1 4.5 collective-permute-start.13
  235.6 5.0 collective-permute-done.17
  248.6 4.5 collective-permute-start.19
  268.2 5.1 collective-permute-start.23
  277.3 7.7 %collective-permute-done.23 = bf16[64,4,4,1]{3,2,1,0:T(4,128)(2,1)S(1)} collective-permute-done((bf16[64,4,4,1]{3,2,1,0:T(4,128)(2,1)S(1)}, bf16[64,4,4,1]{3,2,1,0:T(4,128)(2,1)S(1)}, u32[]{:S(2)}, u32[]{:S(2)}) %collective-permute-start.23) | collective-permute-done | bytes 2080 | tf_op jit(solution)/shard_map/ppermute | solution.py:17
  331.1 4.8 collective-permute-start.25
  372.4 8.4 %all-to-all-start.1 = ((bf16[64,1,1,64]{3,2,1,0:T(2,128)(2,1)}), bf16[64,1,1,64]{3,2,1,0:T(2,128)(2,1)S(1)}, u32[]{:S(2)}, u32[]{:S(2)}) async-start(bf16[64,1,1,64]{3,2,1,0:T(2,128)(2,1)} %constant_dynamic-update-slice_fusion.9), calls=%async_computation.1 | async-start | bytes 65536 | tf_op jit(solution)/shard_map/all_to_all | solution.py:119
  380.8 7.0 %all-to-all-done.1 = bf16[64,1,1,64]{3,2,1,0:T(2,128)(2,1)S(1)} async-done(((bf16[64,1,1,64]{3,2,1,0:T(2,128)(2,1)}), bf16[64,1,1,64]{3,2,1,0:T(2,128)(2,1)S(1)}, u32[]{:S(2)}, u32[]{:S(2)}) %all-to-all-start.1) | async-done | bytes 8224 | tf_op jit(solution)/shard_map/all_to_all | solution.py:119
  388.7 5.6 %all-to-all-start.2 = ((bf16[1,128,64]{2,0,1:T(2,128)(2,1)}), bf16[1,128,64]{2,0,1:T(2,128)(2,1)S(1)}, u32[]{:S(2)}, u32[]{:S(2)}) async-start(bf16[1,128,64]{2,0,1:T(2,128)(2,1)} %copy.369), calls=%async_computation.2 | async-start | bytes 131072 | tf_op jit(solution)/shard_map/all_to_all | solution.py:103
  394.5 7.0 %all-to-all-done.2 = bf16[1,128,64]{2,0,1:T(2,128)(2,1)S(1)} async-done(((bf16[1,128,64]{2,0,1:T(2,128)(2,1)}), bf16[1,128,64]{2,0,1:T(2,128)(2,1)S(1)}, u32[]{:S(2)}, u32[]{:S(2)}) %all-to-all-start.2) | async-done | bytes 16416 | tf_op jit(solution)/shard_map/all_to_all | solution.py:103
  403.5 5.0 collective-permute-start.27
  413.3 12.1 %all_to_all.28 = bf16[64,1,2,64]{3,2,1,0:T(2,128)(2,1)S(1)} all-to-all(bf16[64,1,2,64]{3,2,1,0:T(2,128)(2,1)S(1)} %constant_dynamic-update-slice_fusion.73), channel_id=1, replica_groups=mesh['gx'=16,'gy'=4,'gz'=4] {'gx','gy'}, dimensions={0} | all-to-all | bytes 32768 | tf_op jit(solution)/shard_map/all_to_all | solution.py:119
  427.6 4.5 collective-permute-start.29
  451.0 4.3 collective-permute-start.32
  468.0 4.5 collective-permute-start.35
  482.0 5.6 %collective-permute-done.36 = bf16[96,6,1,256]{0,3,2,1:T(8,128)(2,1)S(1)} collective-permute-done((bf16[96,6,1,256]{0,3,2,1:T(8,128)(2,1)S(1)}, bf16[96,6,1,256]{0,3,2,1:T(8,128)(2,1)S(1)}, u32[]{:S(2)}, u32[]{:S(2)}) %collective-permute-start.36) | collective-permute-done | bytes 294944 | tf_op jit(solution)/shard_map/ppermute | solution.py:15
  492.0 5.5 %collective-permute-start.38 = (bf16[96,6,6,1]{0,3,2,1:T(2,128)(2,1)S(1)}, bf16[96,6,6,1]{0,3,2,1:T(2,128)(2,1)S(1)}, u32[]{:S(2)}, u32[]{:S(2)}) collective-permute-start(bf16[96,6,6,1]{0,3,2,1:T(2,128)(2,1)S(1)} %get-tuple-element.7), channel_id=1, source_target_pairs={{0,1},{1,2},{2,3},{4,5},{5,6},{6,7},{8,9},{9,10},{10,11},{12,13},{... | collective-permute-start | bytes 20744 | tf_op jit(solution)/shard_map/ppermute | solution.py:15
  (699 shorter events, 364.4 us)
Async XLA Ops:
  11.1 8.5 %collective-permute-start.2 = (bf16[32,6,1,256]{3,2,1,0:T(2,128)(2,1)S(1)}, bf16[32,6,1,256]{3,2,1,0:T(2,128)(2,1)S(1)}, u32[]{:S(2)}, u32[]{:S(2)}) collective-permute-start(bf16[32,6,1,256]{3,2,1,0:T(2,128)(2,1)S(1)} %get-tuple-element.157), channel_id=1, source_target_pairs={{0,4},{4,8},{8,12},{1,5},{5,9},{9,13},{2,6},{6,10},{10,14},{3,7},{... | collective-permute-start | bytes 294920 | tf_op jit(solution)/shard_map/ppermute | solution.py:15
  14.5 9.6 %collective-permute-start.3 = (bf16[32,6,1,256]{3,2,1,0:T(2,128)(2,1)S(1)}, bf16[32,6,1,256]{3,2,1,0:T(2,128)(2,1)S(1)}, u32[]{:S(2)}, u32[]{:S(2)}) collective-permute-start(bf16[32,6,1,256]{3,2,1,0:T(2,128)(2,1)S(1)} %get-tuple-element.158), channel_id=1, source_target_pairs={{4,0},{8,4},{12,8},{5,1},{9,5},{13,9},{6,2},{10,6},{14,10},{7,3},{... | collective-permute-start | bytes 294920 | tf_op jit(solution)/shard_map/ppermute | solution.py:17
  25.9 23.8 %collective-permute-start.5 = (bf16[32,6,6,1]{3,2,1,0:T(8,128)(2,1)}, bf16[32,6,6,1]{3,2,1,0:T(8,128)(2,1)}, u32[]{:S(2)}, u32[]{:S(2)}) collective-permute-start(bf16[32,6,6,1]{3,2,1,0:T(8,128)(2,1)} %get-tuple-element.111), channel_id=1, source_target_pairs={{1,0},{2,1},{3,2},{5,4},{6,5},{7,6},{9,8},{10,9},{11,10},{13,12},{... | collective-permute-start | bytes 6920 | tf_op jit(solution)/shard_map/ppermute | solution.py:17
  27.8 22.5 %collective-permute-start.4 = (bf16[32,6,6,1]{3,2,1,0:T(8,128)(2,1)}, bf16[32,6,6,1]{3,2,1,0:T(8,128)(2,1)}, u32[]{:S(2)}, u32[]{:S(2)}) collective-permute-start(bf16[32,6,6,1]{3,2,1,0:T(8,128)(2,1)} %get-tuple-element.112), channel_id=1, source_target_pairs={{0,1},{1,2},{2,3},{4,5},{5,6},{6,7},{8,9},{9,10},{10,11},{12,13},{... | collective-permute-start | bytes 6920 | tf_op jit(solution)/shard_map/ppermute | solution.py:15
  109.3 8.1 %collective-permute-start.8 = (bf16[32,6,1,256]{3,2,1,0:T(2,128)(2,1)S(1)}, bf16[32,6,1,256]{3,2,1,0:T(2,128)(2,1)S(1)}, u32[]{:S(2)}, u32[]{:S(2)}) collective-permute-start(bf16[32,6,1,256]{3,2,1,0:T(2,128)(2,1)S(1)} %get-tuple-element.152), channel_id=1, source_target_pairs={{0,4},{4,8},{8,12},{1,5},{5,9},{9,13},{2,6},{6,10},{10,14},{3,7},{... | collective-permute-start | bytes 294920 | tf_op jit(solution)/shard_map/ppermute | solution.py:15
  112.7 8.8 %collective-permute-start.9 = (bf16[32,6,1,256]{3,2,1,0:T(2,128)(2,1)S(1)}, bf16[32,6,1,256]{3,2,1,0:T(2,128)(2,1)S(1)}, u32[]{:S(2)}, u32[]{:S(2)}) collective-permute-start(bf16[32,6,1,256]{3,2,1,0:T(2,128)(2,1)S(1)} %get-tuple-element.153), channel_id=1, source_target_pairs={{4,0},{8,4},{12,8},{5,1},{9,5},{13,9},{6,2},{10,6},{14,10},{7,3},{... | collective-permute-start | bytes 294920 | tf_op jit(solution)/shard_map/ppermute | solution.py:17
  123.2 20.8 %collective-permute-start.10 = (bf16[32,6,6,1]{3,2,1,0:T(8,128)(2,1)}, bf16[32,6,6,1]{3,2,1,0:T(8,128)(2,1)}, u32[]{:S(2)}, u32[]{:S(2)}) collective-permute-start(bf16[32,6,6,1]{3,2,1,0:T(8,128)(2,1)} %get-tuple-element.107), channel_id=1, source_target_pairs={{0,1},{1,2},{2,3},{4,5},{5,6},{6,7},{8,9},{9,10},{10,11},{12,13},{... | collective-permute-start | bytes 6920 | tf_op jit(solution)/shard_map/ppermute | solution.py:15
  128.8 21.8 %collective-permute-start.11 = (bf16[32,6,6,1]{3,2,1,0:T(8,128)(2,1)}, bf16[32,6,6,1]{3,2,1,0:T(8,128)(2,1)}, u32[]{:S(2)}, u32[]{:S(2)}) collective-permute-start(bf16[32,6,6,1]{3,2,1,0:T(8,128)(2,1)} %get-tuple-element.108), channel_id=1, source_target_pairs={{1,0},{2,1},{3,2},{5,4},{6,5},{7,6},{9,8},{10,9},{11,10},{13,12},{... | collective-permute-start | bytes 6920 | tf_op jit(solution)/shard_map/ppermute | solution.py:17
  227.8 7.9 %collective-permute-start.16 = (bf16[32,4,4,1]{3,0,2,1:T(8,128)(2,1)S(1)}, bf16[32,4,4,1]{3,0,2,1:T(8,128)(2,1)S(1)}, u32[]{:S(2)}, u32[]{:S(2)}) collective-permute-start(bf16[32,4,4,1]{3,0,2,1:T(8,128)(2,1)S(1)} %get-tuple-element.206), channel_id=1, source_target_pairs={{0,1},{1,2},{2,3},{4,5},{5,6},{6,7},{8,9},{9,10},{10,11},{12,13},{... | collective-permute-start | bytes 3080 | tf_op jit(solution)/shard_map/ppermute | solution.py:15
  231.0 9.6 %collective-permute-start.17 = (bf16[32,4,4,1]{3,0,2,1:T(8,128)(2,1)S(1)}, bf16[32,4,4,1]{3,0,2,1:T(8,128)(2,1)S(1)}, u32[]{:S(2)}, u32[]{:S(2)}) collective-permute-start(bf16[32,4,4,1]{3,0,2,1:T(8,128)(2,1)S(1)} %get-tuple-element.207), channel_id=1, source_target_pairs={{1,0},{2,1},{3,2},{5,4},{6,5},{7,6},{9,8},{10,9},{11,10},{13,12},{... | collective-permute-start | bytes 3080 | tf_op jit(solution)/shard_map/ppermute | solution.py:17
  266.2 11.1 %collective-permute-start.22 = (bf16[64,4,4,1]{3,2,1,0:T(4,128)(2,1)}, bf16[64,4,4,1]{3,2,1,0:T(4,128)(2,1)S(1)}, u32[]{:S(2)}, u32[]{:S(2)}) collective-permute-start(bf16[64,4,4,1]{3,2,1,0:T(4,128)(2,1)} %get-tuple-element.169), channel_id=1, source_target_pairs={{0,1},{1,2},{2,3},{4,5},{5,6},{6,7},{8,9},{9,10},{10,11},{12,13},{... | collective-permute-start | bytes 6152 | tf_op jit(solution)/shard_map/ppermute | solution.py:15
  268.2 16.8 %collective-permute-start.23 = (bf16[64,4,4,1]{3,2,1,0:T(4,128)(2,1)S(1)}, bf16[64,4,4,1]{3,2,1,0:T(4,128)(2,1)S(1)}, u32[]{:S(2)}, u32[]{:S(2)}) collective-permute-start(bf16[64,4,4,1]{3,2,1,0:T(4,128)(2,1)S(1)} %get-tuple-element.170), channel_id=1, source_target_pairs={{1,0},{2,1},{3,2},{5,4},{6,5},{7,6},{9,8},{10,9},{11,10},{13,12},{... | collective-permute-start | bytes 6152 | tf_op jit(solution)/shard_map/ppermute | solution.py:17
  306.7 22.4 %all-to-all-start = ((bf16[1,64,64]{2,0,1:T(2,128)(2,1)}), bf16[1,64,64]{2,0,1:T(2,128)(2,1)S(1)}, u32[]{:S(2)}, u32[]{:S(2)}) async-start(bf16[1,64,64]{2,0,1:T(2,128)(2,1)} %copy.368), calls=%async_computation | async-start | bytes 65536 | tf_op jit(solution)/shard_map/all_to_all | solution.py:103
  372.4 15.4 %all-to-all-start.1 = ((bf16[64,1,1,64]{3,2,1,0:T(2,128)(2,1)}), bf16[64,1,1,64]{3,2,1,0:T(2,128)(2,1)S(1)}, u32[]{:S(2)}, u32[]{:S(2)}) async-start(bf16[64,1,1,64]{3,2,1,0:T(2,128)(2,1)} %constant_dynamic-update-slice_fusion.9), calls=%async_computation.1 | async-start | bytes 65536 | tf_op jit(solution)/shard_map/all_to_all | solution.py:119
  388.7 12.7 %all-to-all-start.2 = ((bf16[1,128,64]{2,0,1:T(2,128)(2,1)}), bf16[1,128,64]{2,0,1:T(2,128)(2,1)S(1)}, u32[]{:S(2)}, u32[]{:S(2)}) async-start(bf16[1,128,64]{2,0,1:T(2,128)(2,1)} %copy.369), calls=%async_computation.2 | async-start | bytes 131072 | tf_op jit(solution)/shard_map/all_to_all | solution.py:103
  403.5 8.3 %collective-permute-start.27 = (bf16[2,16,4,1]{3,1,2,0:T(8,128)(2,1)S(1)}, bf16[2,16,4,1]{3,1,2,0:T(8,128)(2,1)S(1)}, u32[]{:S(2)}, u32[]{:S(2)}) collective-permute-start(bf16[2,16,4,1]{3,1,2,0:T(8,128)(2,1)S(1)} %get-tuple-element.290), channel_id=1, source_target_pairs={{1,0},{2,1},{3,2},{5,4},{6,5},{7,6},{9,8},{10,9},{11,10},{13,12},{... | collective-permute-start | bytes 776 | tf_op jit(solution)/shard_map/ppermute | solution.py:17
  434.8 8.3 %collective-permute-start.30 = (bf16[192,4,1,128]{0,3,2,1:T(8,128)(2,1)S(1)}, bf16[192,4,1,128]{0,3,2,1:T(8,128)(2,1)S(1)}, u32[]{:S(2)}, u32[]{:S(2)}) collective-permute-start(bf16[192,4,1,128]{0,3,2,1:T(8,128)(2,1)S(1)} %get-tuple-element.127), channel_id=1, source_target_pairs={{0,4},{4,8},{8,12},{1,5},{5,9},{9,13},{2,6},{6,10},{10,14},{3,7},{... | collective-permute-start | bytes 589832 | tf_op jit(solution)/shard_map/ppermute | solution.py:15
  437.3 10.0 %collective-permute-start.31 = (bf16[192,4,1,128]{0,3,2,1:T(8,128)(2,1)S(1)}, bf16[192,4,1,128]{0,3,2,1:T(8,128)(2,1)S(1)}, u32[]{:S(2)}, u32[]{:S(2)}) collective-permute-start(bf16[192,4,1,128]{0,3,2,1:T(8,128)(2,1)S(1)} %get-tuple-element.128), channel_id=1, source_target_pairs={{4,0},{8,4},{12,8},{5,1},{9,5},{13,9},{6,2},{10,6},{14,10},{7,3},{... | collective-permute-start | bytes 589832 | tf_op jit(solution)/shard_map/ppermute | solution.py:17
  447.3 8.6 %collective-permute-start.33 = (bf16[192,4,4,1]{0,2,3,1:T(4,128)(2,1)S(1)}, bf16[192,4,4,1]{0,2,3,1:T(4,128)(2,1)S(1)}, u32[]{:S(2)}, u32[]{:S(2)}) collective-permute-start(bf16[192,4,4,1]{0,2,3,1:T(4,128)(2,1)S(1)} %copy.377), channel_id=1, source_target_pairs={{1,0},{2,1},{3,2},{5,4},{6,5},{7,6},{9,8},{10,9},{11,10},{13,12},{... | collective-permute-start | bytes 18440 | tf_op jit(solution)/shard_map/ppermute | solution.py:17
  466.0 9.5 %collective-permute-start.34 = (bf16[96,1,4,256]{0,3,2,1:T(8,128)(2,1)S(1)}, bf16[96,1,4,256]{0,3,2,1:T(8,128)(2,1)S(1)}, u32[]{:S(2)}, u32[]{:S(2)}) collective-permute-start(bf16[96,1,4,256]{0,3,2,1:T(8,128)(2,1)S(1)} %get-tuple-element.33), channel_id=1, source_target_pairs={{0,16},{16,32},{32,48},{48,64},{64,80},{80,96},{96,112},{112,128},... | collective-permute-start | bytes 589832 | tf_op jit(solution)/shard_map/ppermute | solution.py:15
  468.0 8.4 %collective-permute-start.35 = (bf16[96,1,4,256]{0,3,2,1:T(8,128)(2,1)S(1)}, bf16[96,1,4,256]{0,3,2,1:T(8,128)(2,1)S(1)}, u32[]{:S(2)}, u32[]{:S(2)}) collective-permute-start(bf16[96,1,4,256]{0,3,2,1:T(8,128)(2,1)S(1)} %get-tuple-element.34), channel_id=1, source_target_pairs={{16,0},{32,16},{48,32},{64,48},{80,64},{96,80},{112,96},{128,112},... | collective-permute-start | bytes 589832 | tf_op jit(solution)/shard_map/ppermute | solution.py:17
  476.7 10.9 %collective-permute-start.36 = (bf16[96,6,1,256]{0,3,2,1:T(8,128)(2,1)S(1)}, bf16[96,6,1,256]{0,3,2,1:T(8,128)(2,1)S(1)}, u32[]{:S(2)}, u32[]{:S(2)}) collective-permute-start(bf16[96,6,1,256]{0,3,2,1:T(8,128)(2,1)S(1)} %get-tuple-element.11), channel_id=1, source_target_pairs={{0,4},{4,8},{8,12},{1,5},{5,9},{9,13},{2,6},{6,10},{10,14},{3,7},{... | collective-permute-start | bytes 884744 | tf_op jit(solution)/shard_map/ppermute | solution.py:15
  479.3 12.6 %collective-permute-start.37 = (bf16[96,6,1,256]{0,3,2,1:T(8,128)(2,1)S(1)}, bf16[96,6,1,256]{0,3,2,1:T(8,128)(2,1)S(1)}, u32[]{:S(2)}, u32[]{:S(2)}) collective-permute-start(bf16[96,6,1,256]{0,3,2,1:T(8,128)(2,1)S(1)} %get-tuple-element.12), channel_id=1, source_target_pairs={{4,0},{8,4},{12,8},{5,1},{9,5},{13,9},{6,2},{10,6},{14,10},{7,3},{... | collective-permute-start | bytes 884744 | tf_op jit(solution)/shard_map/ppermute | solution.py:17
  492.0 12.1 %collective-permute-start.38 = (bf16[96,6,6,1]{0,3,2,1:T(2,128)(2,1)S(1)}, bf16[96,6,6,1]{0,3,2,1:T(2,128)(2,1)S(1)}, u32[]{:S(2)}, u32[]{:S(2)}) collective-permute-start(bf16[96,6,6,1]{0,3,2,1:T(2,128)(2,1)S(1)} %get-tuple-element.7), channel_id=1, source_target_pairs={{0,1},{1,2},{2,3},{4,5},{5,6},{6,7},{8,9},{9,10},{10,11},{12,13},{... | collective-permute-start | bytes 20744 | tf_op jit(solution)/shard_map/ppermute | solution.py:15
  (74 other events, 1087.5 us)
